TPU v7x, 32 devices: a whole 2x2x4 slice. The times are simulated.
32 devices in a mesh: gx: 4 (over x, core), gy: 8 (over z, y).
Axes of the slice: x: 2, y: 2, z: 4, core: 2. Of those that a mesh axis runs over, the one named last changes fastest.
Arguments:
- green_ops: bfloat16 [4, 8, 2, 1024, 1024], P('gx', 'gy'), may hold values from -0.125 to 0.125
- cell_map: int32 [4, 8, 1024], P('gx', 'gy'), may hold values from 0 to 2
- dipole_site: int32 [4, 8, 128], P('gx', 'gy'), may hold values from 0 to 1023
- dipole_amp: float32 [4, 8, 2, 128], P('gx', 'gy'), may hold values from -32 to 32
- contrast: float32 [3, 2], replicated, may hold values from 0.3 to 1
Outputs:
- traces: bfloat16 [4, 8, 1024, 2, 128], P('gx', 'gy')
All inputs are finite; a program needn't handle non-finite values.
Results may differ from a plain program's by a relative error of at most 0.0069.
Values may be sent and summed in bfloat16 or wider, within the bound.
A program may use at most 64 MiB of HBM per device.

v0:
```python
import jax
import jax.numpy as jnp
from jax import lax
from jax.sharding import PartitionSpec as P

NB = 64
MB = 2
STEPS = 4


def from_behind(block, axis, distance):
    devices = range(lax.axis_size(axis))
    route = [(i - distance, i) for i in devices if i - distance in devices]
    return lax.ppermute(block, axis, route)


def combine(product):
    real_out = product[0, :, 0] - product[1, :, 1]
    imag_out = product[0, :, 1] + product[1, :, 0]
    return jnp.stack([real_out, imag_out], axis=1).astype(jnp.bfloat16)


def per_device(green_ops, cell_map, dipole_site, dipole_amp, contrast):
    operator = green_ops[0, 0]
    cells = cell_map[0, 0]
    sites = dipole_site[0, 0]
    amplitude = dipole_amp[0, 0]
    trace_rows = operator.shape[1]
    face_rows = trace_rows // 2
    columns = sites.shape[0]
    one_hot = (lax.broadcasted_iota(jnp.int32, (trace_rows, columns), 0) == sites[None, :]).astype(
        jnp.float32
    )
    source = one_hot[:, None, :] * amplitude[None, :, :]
    lookup_table = (
        lax.broadcasted_iota(jnp.int32, (trace_rows, contrast.shape[0]), 1) == cells[:, None]
    ).astype(jnp.float32)
    factor = jnp.dot(lookup_table, contrast, precision=lax.Precision.HIGHEST)
    real_factor = factor[:, 0:1]
    imag_factor = factor[:, 1:2]
    east_trace = jnp.zeros((face_rows, 2, 0), jnp.bfloat16)
    north_trace = jnp.zeros((face_rows, 2, 0), jnp.bfloat16)
    for turn_index in range(STEPS):
        width_live = min(turn_index + 1, MB) * NB
        width_held = east_trace.shape[2]
        if width_held > 0:
            west_trace = from_behind(east_trace, "gx", 1)
            south_trace = from_behind(north_trace, "gy", 1)
        else:
            west_trace = east_trace
            south_trace = north_trace
        padding = ((0, 0), (0, 0), (0, width_live - width_held))
        west_trace = jnp.pad(west_trace, padding)
        south_trace = jnp.pad(south_trace, padding)
        incoming = jnp.concatenate([west_trace, south_trace], axis=0).astype(jnp.float32)
        real_in = (
            real_factor * incoming[:, 0] - imag_factor * incoming[:, 1] + source[:, 0, :width_live]
        )
        imag_in = (
            real_factor * incoming[:, 1] + imag_factor * incoming[:, 0] + source[:, 1, :width_live]
        )
        excited = jnp.stack([real_in, imag_in], axis=1).astype(jnp.bfloat16)
        image_width_live = excited.shape[2]
        flat = excited.reshape(trace_rows, 2 * image_width_live)
        product = jnp.einsum("spq,qc->spc", operator, flat, preferred_element_type=jnp.float32)
        image = combine(product.reshape(2, trace_rows - 0, 2, image_width_live))
        east_trace = image[:face_rows]
        north_trace = image[face_rows:]
    padding = ((0, 0), (0, 0), (0, columns - east_trace.shape[2]))
    traces = jnp.concatenate([east_trace, north_trace], axis=0)
    return traces[None, None]


def solution(mesh):
    placed = (
        P("gx", "gy", None, None, None),
        P("gx", "gy", None),
        P("gx", "gy", None),
        P("gx", "gy", None, None),
        P(),
    )
    return jax.shard_map(
        per_device,
        mesh=mesh,
        in_specs=placed,
        out_specs=P("gx", "gy", None, None, None),
        check_vma=False,
    )
```

profile of v0, /device:TPU:8, one launch (start us, length us, event | category | flops | bytes accessed | tf_op | source)
XLA Modules:
  0.0 52.5 jit_solution(15152562998942121899)
XLA Ops:
  0.0 0.0 copy-start
  0.0 0.7 %copy-done = f32[3,2]{0,1:T(2,128)S(1)} copy-done((f32[3,2]{0,1:T(2,128)S(1)}, f32[3,2]{0,1:T(2,128)}, u32[]{:S(2)}) %copy-start) | copy-done | bytes 48
  0.7 1.1 %fusion.17 = f32[1024,2]{0,1:T(2,128)S(1)} fusion(f32[3,2]{0,1:T(2,128)S(1)} %copy-done, s32[1024]{0:T(1024)} %bitcast.77), kind=kOutput, calls=%fused_computation.44 | convolution fusion | flops 76800 | bytes 12312 | tf_op jit(solution)/shard_map/dot_general | solution.py:38
  1.8 0.8 %fusion.16 = f32[1024,128]{0,1:T(8,128)S(1)} fusion(s32[128]{0:T(128)} %bitcast.76), kind=kLoop, calls=%fused_computation.43 | loop fusion | flops 262144 | bytes 524800 | tf_op jit(solution)/shard_map/convert_element_type | solution.py:31
  2.6 0.8 %broadcast_multiply_fusion = f32[1024,2,128]{0,2,1:T(8,128)S(1)} fusion(f32[2,128]{1,0:T(2,128)} %bitcast.75, f32[1024,128]{0,1:T(8,128)S(1)} %fusion.16), kind=kLoop, calls=%fused_computation.40 | loop fusion | flops 262144 | bytes 1573888 | tf_op jit(solution)/shard_map/mul | solution.py:34
  3.5 3.7 %fusion.6 = f32[128,2,1024]{2,0,1:T(8,128)S(1)} fusion(bf16[1024,128,1]{0,1,2:T(8,128)(2,1)S(1)} %bitcast.63, bf16[1,1,2,1024,1024]{4,3,2,1,0:T(8,128)(2,1)} %param.5), kind=kOutput, calls=%fused_computation.6 | convolution fusion | flops 536870912 | bytes 5505024 | tf_op jit(solution)/shard_map/spq,qc->spc/dot_general | solution.py:65
  7.2 0.0 copy-start.1
  7.3 0.1 fusion.32
  7.4 2.0 %collective-permute-start = (bf16[512,2,64]{0,2,1:T(8,128)(2,1)S(1)}, bf16[512,2,64]{0,2,1:T(8,128)(2,1)S(1)}, u32[]{:S(2)}, u32[]{:S(2)}) collective-permute-start(bf16[512,2,64]{0,2,1:T(8,128)(2,1)S(1)} %get-tuple-element.27), channel_id=1, source_target_pairs={{0,8},{8,16},{16,24},{1,9},{9,17},{17,25},{2,10},{10,18},{18,26},{... | collective-permute-start | bytes 393224 | tf_op jit(solution)/shard_map/ppermute | solution.py:14
  9.4 3.4 %collective-permute-start.1 = (bf16[512,2,64]{0,2,1:T(8,128)(2,1)S(1)}, bf16[512,2,64]{0,2,1:T(8,128)(2,1)S(1)}, u32[]{:S(2)}, u32[]{:S(2)}) collective-permute-start(bf16[512,2,64]{0,2,1:T(8,128)(2,1)S(1)} %get-tuple-element.28), channel_id=1, source_target_pairs={{0,1},{1,2},{2,3},{3,4},{4,5},{5,6},{6,7},{8,9},{9,10},{10,11},{11... | collective-permute-start | bytes 393224 | tf_op jit(solution)/shard_map/ppermute | solution.py:14
  12.8 0.0 collective-permute-done
  12.8 4.9 %collective-permute-done.1 = bf16[512,2,64]{0,2,1:T(8,128)(2,1)S(1)} collective-permute-done((bf16[512,2,64]{0,2,1:T(8,128)(2,1)S(1)}, bf16[512,2,64]{0,2,1:T(8,128)(2,1)S(1)}, u32[]{:S(2)}, u32[]{:S(2)}) %collective-permute-start.1) | collective-permute-done | bytes 131104 | tf_op jit(solution)/shard_map/ppermute | solution.py:14
  17.7 0.1 fusion.11
  17.8 0.2 add_convert_fusion.6
  18.1 0.1 pad_maximum_fusion
  18.2 0.0 copy-done.1
  18.2 1.3 %fusion.4 = f32[256,2,1024]{2,0,1:T(8,128)S(1)} fusion(bf16[1024,256,1]{0,1,2:T(8,128)(2,1)S(1)} %bitcast.64, bf16[1,1,2,1024,1024]{4,3,2,1,0:T(8,128)(2,1)S(1)} %copy-done.1), kind=kOutput, calls=%fused_computation.4 | convolution fusion | flops 1073741824 | bytes 6815744 | tf_op jit(solution)/shard_map/spq,qc->spc/dot_general | solution.py:65
  19.5 0.1 fusion.22
  19.6 2.5 %collective-permute-start.2 = (bf16[512,2,128]{0,2,1:T(8,128)(2,1)S(1)}, bf16[512,2,128]{0,2,1:T(8,128)(2,1)S(1)}, u32[]{:S(2)}, u32[]{:S(2)}) collective-permute-start(bf16[512,2,128]{0,2,1:T(8,128)(2,1)S(1)} %get-tuple-element.25), channel_id=1, source_target_pairs={{0,8},{8,16},{16,24},{1,9},{9,17},{17,25},{2,10},{10,18},{18,26},{... | collective-permute-start | bytes 786440 | tf_op jit(solution)/shard_map/ppermute | solution.py:14
  22.2 2.5 %collective-permute-start.3 = (bf16[512,2,128]{0,2,1:T(8,128)(2,1)S(1)}, bf16[512,2,128]{0,2,1:T(8,128)(2,1)S(1)}, u32[]{:S(2)}, u32[]{:S(2)}) collective-permute-start(bf16[512,2,128]{0,2,1:T(8,128)(2,1)S(1)} %get-tuple-element.26), channel_id=1, source_target_pairs={{0,1},{1,2},{2,3},{3,4},{4,5},{5,6},{6,7},{8,9},{9,10},{10,11},{11... | collective-permute-start | bytes 786440 | tf_op jit(solution)/shard_map/ppermute | solution.py:14
  24.7 0.0 collective-permute-done.2
  24.7 9.0 %collective-permute-done.3 = bf16[512,2,128]{0,2,1:T(8,128)(2,1)S(1)} collective-permute-done((bf16[512,2,128]{0,2,1:T(8,128)(2,1)S(1)}, bf16[512,2,128]{0,2,1:T(8,128)(2,1)S(1)}, u32[]{:S(2)}, u32[]{:S(2)}) %collective-permute-start.3) | collective-permute-done | bytes 262176 | tf_op jit(solution)/shard_map/ppermute | solution.py:14
  33.7 0.1 maximum_convert_fusion
  33.9 0.2 add_convert_fusion.4
  34.1 0.1 pad_maximum_fusion.1
  34.2 1.3 %fusion.2 = f32[256,2,1024]{2,0,1:T(8,128)S(1)} fusion(bf16[1024,256,1]{0,1,2:T(8,128)(2,1)S(1)} %bitcast.65, bf16[1,1,2,1024,1024]{4,3,2,1,0:T(8,128)(2,1)S(1)} %copy-done.1), kind=kOutput, calls=%fused_computation.2 | convolution fusion | flops 1073741824 | bytes 6815744 | tf_op jit(solution)/shard_map/spq,qc->spc/dot_general | solution.py:65
  35.5 0.1 fusion.24
  35.7 1.6 %collective-permute-start.4 = (bf16[512,2,128]{0,2,1:T(8,128)(2,1)S(1)}, bf16[512,2,128]{0,2,1:T(8,128)(2,1)S(1)}, u32[]{:S(2)}, u32[]{:S(2)}) collective-permute-start(bf16[512,2,128]{0,2,1:T(8,128)(2,1)S(1)} %get-tuple-element.23), channel_id=1, source_target_pairs={{0,8},{8,16},{16,24},{1,9},{9,17},{17,25},{2,10},{10,18},{18,26},{... | collective-permute-start | bytes 786440 | tf_op jit(solution)/shard_map/ppermute | solution.py:14
  37.3 1.9 %collective-permute-start.5 = (bf16[512,2,128]{0,2,1:T(8,128)(2,1)S(1)}, bf16[512,2,128]{0,2,1:T(8,128)(2,1)S(1)}, u32[]{:S(2)}, u32[]{:S(2)}) collective-permute-start(bf16[512,2,128]{0,2,1:T(8,128)(2,1)S(1)} %get-tuple-element.24), channel_id=1, source_target_pairs={{0,1},{1,2},{2,3},{3,4},{4,5},{5,6},{6,7},{8,9},{9,10},{10,11},{11... | collective-permute-start | bytes 786440 | tf_op jit(solution)/shard_map/ppermute | solution.py:14
  39.2 0.0 collective-permute-done.4
  39.2 9.1 %collective-permute-done.5 = bf16[512,2,128]{0,2,1:T(8,128)(2,1)S(1)} collective-permute-done((bf16[512,2,128]{0,2,1:T(8,128)(2,1)S(1)}, bf16[512,2,128]{0,2,1:T(8,128)(2,1)S(1)}, u32[]{:S(2)}, u32[]{:S(2)}) %collective-permute-start.5) | collective-permute-done | bytes 262176 | tf_op jit(solution)/shard_map/ppermute | solution.py:14
  48.3 0.1 maximum_convert_fusion.1
  48.4 0.2 add_convert_fusion.2
  48.6 0.1 pad_maximum_fusion.2
  48.7 1.3 %fusion = f32[256,2,1024]{2,0,1:T(8,128)S(1)} fusion(bf16[1024,256,1]{0,1,2:T(8,128)(2,1)S(1)} %bitcast.66, bf16[1,1,2,1024,1024]{4,3,2,1,0:T(8,128)(2,1)S(1)} %copy-done.1), kind=kOutput, calls=%fused_computation | convolution fusion | flops 1073741824 | bytes 6815744 | tf_op jit(solution)/shard_map/spq,qc->spc/dot_general | solution.py:65
  50.0 0.1 fusion.36
  50.1 0.2 copy.16
  50.3 0.2 copy.17
  50.5 0.2 copy.15
  50.8 0.2 copy.18
  51.0 0.1 fusion.18
  51.1 0.1 pad_maximum_fusion.3
  51.1 1.3 %copy.14 = bf16[1,1,1024,2,128]{4,3,2,1,0:T(2,128)(2,1)} copy(bf16[1,1,1024,2,128]{4,2,3,1,0:T(8,128)(2,1)S(1)} %pad_maximum_fusion.3) | data formatting | bytes 1048576 | tf_op jit(solution)/shard_map/stack | solution.py:20
  (8 shorter events, 0.2 us)
Async XLA Ops:
  0.0 0.7 %copy-start = (f32[3,2]{0,1:T(2,128)S(1)}, f32[3,2]{0,1:T(2,128)}, u32[]{:S(2)}) copy-start(f32[3,2]{0,1:T(2,128)} %param.9) | copy-start | bytes 76
  7.2 10.9 %copy-start.1 = (bf16[1,1,2,1024,1024]{4,3,2,1,0:T(8,128)(2,1)S(1)}, bf16[1,1,2,1024,1024]{4,3,2,1,0:T(8,128)(2,1)}, u32[]{:S(2)}) copy-start(bf16[1,1,2,1024,1024]{4,3,2,1,0:T(8,128)(2,1)} %param.5) | copy-start | bytes 12582916
  7.4 5.5 %collective-permute-start = (bf16[512,2,64]{0,2,1:T(8,128)(2,1)S(1)}, bf16[512,2,64]{0,2,1:T(8,128)(2,1)S(1)}, u32[]{:S(2)}, u32[]{:S(2)}) collective-permute-start(bf16[512,2,64]{0,2,1:T(8,128)(2,1)S(1)} %get-tuple-element.27), channel_id=1, source_target_pairs={{0,8},{8,16},{16,24},{1,9},{9,17},{17,25},{2,10},{10,18},{18,26},{... | collective-permute-start | bytes 393224 | tf_op jit(solution)/shard_map/ppermute | solution.py:14
  9.4 8.4 %collective-permute-start.1 = (bf16[512,2,64]{0,2,1:T(8,128)(2,1)S(1)}, bf16[512,2,64]{0,2,1:T(8,128)(2,1)S(1)}, u32[]{:S(2)}, u32[]{:S(2)}) collective-permute-start(bf16[512,2,64]{0,2,1:T(8,128)(2,1)S(1)} %get-tuple-element.28), channel_id=1, source_target_pairs={{0,1},{1,2},{2,3},{3,4},{4,5},{5,6},{6,7},{8,9},{9,10},{10,11},{11... | collective-permute-start | bytes 393224 | tf_op jit(solution)/shard_map/ppermute | solution.py:14
  19.6 5.1 %collective-permute-start.2 = (bf16[512,2,128]{0,2,1:T(8,128)(2,1)S(1)}, bf16[512,2,128]{0,2,1:T(8,128)(2,1)S(1)}, u32[]{:S(2)}, u32[]{:S(2)}) collective-permute-start(bf16[512,2,128]{0,2,1:T(8,128)(2,1)S(1)} %get-tuple-element.25), channel_id=1, source_target_pairs={{0,8},{8,16},{16,24},{1,9},{9,17},{17,25},{2,10},{10,18},{18,26},{... | collective-permute-start | bytes 786440 | tf_op jit(solution)/shard_map/ppermute | solution.py:14
  22.2 11.5 %collective-permute-start.3 = (bf16[512,2,128]{0,2,1:T(8,128)(2,1)S(1)}, bf16[512,2,128]{0,2,1:T(8,128)(2,1)S(1)}, u32[]{:S(2)}, u32[]{:S(2)}) collective-permute-start(bf16[512,2,128]{0,2,1:T(8,128)(2,1)S(1)} %get-tuple-element.26), channel_id=1, source_target_pairs={{0,1},{1,2},{2,3},{3,4},{4,5},{5,6},{6,7},{8,9},{9,10},{10,11},{11... | collective-permute-start | bytes 786440 | tf_op jit(solution)/shard_map/ppermute | solution.py:14
  35.7 3.5 %collective-permute-start.4 = (bf16[512,2,128]{0,2,1:T(8,128)(2,1)S(1)}, bf16[512,2,128]{0,2,1:T(8,128)(2,1)S(1)}, u32[]{:S(2)}, u32[]{:S(2)}) collective-permute-start(bf16[512,2,128]{0,2,1:T(8,128)(2,1)S(1)} %get-tuple-element.23), channel_id=1, source_target_pairs={{0,8},{8,16},{16,24},{1,9},{9,17},{17,25},{2,10},{10,18},{18,26},{... | collective-permute-start | bytes 786440 | tf_op jit(solution)/shard_map/ppermute | solution.py:14
  37.3 11.0 %collective-permute-start.5 = (bf16[512,2,128]{0,2,1:T(8,128)(2,1)S(1)}, bf16[512,2,128]{0,2,1:T(8,128)(2,1)S(1)}, u32[]{:S(2)}, u32[]{:S(2)}) collective-permute-start(bf16[512,2,128]{0,2,1:T(8,128)(2,1)S(1)} %get-tuple-element.24), channel_id=1, source_target_pairs={{0,1},{1,2},{2,3},{3,4},{4,5},{5,6},{6,7},{8,9},{9,10},{10,11},{11... | collective-permute-start | bytes 786440 | tf_op jit(solution)/shard_map/ppermute | solution.py:14
where the time goes:
time: 52.8 us; the launch traced here: 52.5 us
  waiting for transfers between devices  23 us (44%)
  starting transfers between devices  14 us (27%)
  matrix products  8.72 us (17%)
  other arithmetic  3.43 us (6%)
  local copies, waits for them, and re-layouts  2.95 us (6%)
    ppermute x6, waiting for transfers between devices, from_behind(): return lax.ppermute(block, axis, route)  23 us
    ppermute x6, starting transfers between devices, from_behind(): return lax.ppermute(block, axis, route)  14 us
    dot_general x4, matrix products, per_device(): jnp.einsum('spq,qc->spc', operator, flat, preferred_element_type=jnp.floa...  7.59 us
    unnamed x8, local copies, waits for them, and re-layouts  1.46 us
    another operation x1, local copies, waits for them, and re-layouts, combine(): return jnp.stack([real_out, imag_out], axis=1).astype(jnp.bfloat16)  1.33 us
    dot_general x1, matrix products, per_device(): factor = jnp.dot(lookup_table, contrast, precision=lax.Precision.HIGHEST)  1.13 us
  transfers between devices with their start and end apart: 6, of which 3 were waited for; matrix products, arithmetic and copies ran while one was open for 0% of the time, Pallas kernels for 0%

commit v1 on v0

v1 whole, which is shorter than its diff:
```python
import functools

import jax
import jax.numpy as jnp
from jax import lax
from jax.experimental import pallas as pl
from jax.experimental.pallas import tpu as pltpu
from jax.sharding import PartitionSpec as P

MB = 2
STEPS = 4
CHUNKS = 2
TURNS = MB * STEPS - 1
SENDS = TURNS - MB
MESH = pl.DeviceIdType.MESH


def kernel(
    nx, ny, ops_hbm, cells_hbm, site_hbm, amp_hbm, contrast_hbm, out_ref,
    ops, cells, site, amp, contrast, site_of, amp_of, fac, excited, west, south, east_out, north_out, last_b, wide,
    ops_sem, small_sem, send_sem, recv_sem,
):
    i = lax.axis_index("gx")
    j = lax.axis_index("gy")
    rows = ops.shape[1]
    face = rows // 2
    lanes = site.shape[1]
    nb = lanes // 2
    piece = face // CHUNKS

    def ops_copy(k):
        block = pl.ds(face if k == 0 else 0, face)
        return pltpu.make_async_copy(ops_hbm.at[:, block], ops.at[:, block], ops_sem.at[k])

    small = [
        pltpu.make_async_copy(src, dst, small_sem.at[k])
        for k, (src, dst) in enumerate(
            [(site_hbm, site), (amp_hbm, amp), (cells_hbm, cells), (contrast_hbm, contrast)]
        )
    ]
    for copy in small:
        copy.start()
    ops_copy(0).start()
    ops_copy(1).start()

    barrier = pltpu.get_barrier_semaphore()

    @pl.when(i > 0)
    def _():
        pl.semaphore_signal(barrier, inc=1, device_id={"gx": i - 1}, device_id_type=MESH)

    @pl.when(j > 0)
    def _():
        pl.semaphore_signal(barrier, inc=1, device_id={"gy": j - 1}, device_id_type=MESH)

    for copy in small:
        copy.wait()

    low = lax.broadcasted_iota(jnp.int32, (1, lanes), 1) < nb
    sites = site[...]
    sites_turned = pltpu.roll(sites, nb, axis=1)
    site_of[0] = jnp.where(low, sites, sites_turned)
    site_of[1] = jnp.where(low, sites_turned, sites)
    real, imag = amp[0:1, :], amp[1:2, :]
    real_turned, imag_turned = pltpu.roll(real, nb, axis=1), pltpu.roll(imag, nb, axis=1)
    amp_of[0, 0] = jnp.where(low, real, imag_turned)
    amp_of[1, 0] = jnp.where(low, real_turned, imag)
    amp_of[0, 1] = jnp.where(low, -imag, real_turned)
    amp_of[1, 1] = jnp.where(low, -imag_turned, real)

    classes = contrast.shape[1]
    for a in range(rows // lanes):
        column = jnp.broadcast_to(cells[a : a + 1, :], (lanes, lanes)).T
        for c in range(2):
            value = jnp.full((lanes, lanes), contrast[c, 0], jnp.float32)
            for k in range(1, classes):
                value = jnp.where(column == k, contrast[c, k], value)
            fac[c, pl.ds(a * lanes, lanes), :] = value

    @pl.when(i == 0)
    def _():
        west[...] = jnp.zeros_like(west)

    @pl.when(j == 0)
    def _():
        south[...] = jnp.zeros_like(south)

    targets = jnp.where(i < nx - 1, 1, 0) + jnp.where(j < ny - 1, 1, 0)

    @pl.when(targets > 0)
    def _():
        pl.semaphore_wait(barrier, targets)

    def send(direction, turn, part):
        block = pl.ds(part * piece, piece)
        source, target, to = (
            (north_out, south, {"gy": j + 1}) if direction == 0 else (east_out, west, {"gx": i + 1})
        )
        return pltpu.make_async_remote_copy(
            src_ref=source.at[turn, block],
            dst_ref=target.at[turn, block],
            send_sem=send_sem.at[direction, turn, part],
            recv_sem=recv_sem.at[direction, turn, part],
            device_id=to,
            device_id_type=MESH,
        )

    has_target = (j < ny - 1, i < nx - 1)
    has_source = (j > 0, i > 0)

    def source_term(m, offset, size):
        points = lax.broadcasted_iota(jnp.int32, (size, lanes), 0) + offset
        hit = points == site_of[m]
        return (
            jnp.where(hit, amp_of[m, 0], 0.0),
            jnp.where(hit, amp_of[m, 1], 0.0),
        )

    def turn_body(turn, _):
        m = turn % MB

        @pl.when(turn < MB)
        def _():
            for a in range(rows // piece):
                block = pl.ds(a * piece, piece)
                y, iy = source_term(m, a * piece, piece)
                excited[0, block, :] = y.astype(jnp.bfloat16)
                excited[1, block, :] = iy.astype(jnp.bfloat16)

        @pl.when(turn >= MB)
        def _():
            for direction, buffer, base in ((1, west, 0), (0, south, face)):
                for part in range(CHUNKS):
                    @pl.when(has_source[direction])
                    def _():
                        send(direction, turn - MB, part).wait_recv()

                    offset = base + part * piece
                    x = buffer[turn - MB, pl.ds(part * piece, piece), :].astype(jnp.float32)
                    turned = pltpu.roll(x, nb, axis=1)
                    ix = jnp.where(low, -turned, turned)
                    y0, iy0 = source_term(m, offset, piece)
                    block = pl.ds(offset, piece)
                    fr, fi = fac[0, block, :], fac[1, block, :]
                    excited[0, block, :] = (fr * x + fi * ix + y0).astype(jnp.bfloat16)
                    excited[1, block, :] = (fr * ix - fi * x + iy0).astype(jnp.bfloat16)

        for direction, base in ((0, face), (1, 0)):
            @pl.when(turn == 0)
            def _():
                ops_copy(direction).wait()

            for part in range(CHUNKS):
                block = pl.ds(base + part * piece, piece)
                image = jnp.dot(
                    ops[0, block, :], excited[0], preferred_element_type=jnp.float32
                ) + jnp.dot(ops[1, block, :], excited[1], preferred_element_type=jnp.float32)

                @pl.when(turn < SENDS)
                def _():
                    held = north_out if direction == 0 else east_out
                    held[turn, pl.ds(part * piece, piece), :] = image.astype(jnp.bfloat16)

                    @pl.when(has_target[direction])
                    def _():
                        send(direction, turn, part).start()

                @pl.when(turn == TURNS - 2)
                def _():
                    last_b[block, :] = image

                @pl.when(turn == TURNS - 1)
                def _():
                    other = last_b[block, :]
                    start = 2 * (base + part * piece)
                    wide[pl.ds(start, piece, stride=2), :] = jnp.where(
                        low, image, pltpu.roll(other, nb, axis=1)
                    )
                    wide[pl.ds(start + 1, piece, stride=2), :] = jnp.where(
                        low, pltpu.roll(image, nb, axis=1), other
                    )
                    both = pl.ds(start, 2 * piece)
                    out_ref[both, :] = wide[both, :].astype(jnp.bfloat16)

        return 0

    lax.fori_loop(0, TURNS, turn_body, 0)

    for direction in (0, 1):
        @pl.when(has_target[direction])
        def _():
            for turn in range(SENDS):
                for part in range(CHUNKS):
                    send(direction, turn, part).wait_send()


def per_device(nx, ny, green_ops, cell_map, dipole_site, dipole_amp, contrast):
    rows = green_ops.shape[-1]
    lanes = dipole_site.shape[-1]
    face = rows // 2
    bf16, f32, i32 = jnp.bfloat16, jnp.float32, jnp.int32
    out = pl.pallas_call(
        functools.partial(kernel, nx, ny),
        out_shape=jax.ShapeDtypeStruct((2 * rows, lanes), bf16),
        in_specs=[pl.BlockSpec(memory_space=pl.ANY)] * 5,
        out_specs=pl.BlockSpec(memory_space=pltpu.VMEM),
        scratch_shapes=[
            pltpu.VMEM((2, rows, rows), bf16),
            pltpu.VMEM((rows // lanes, lanes), i32),
            pltpu.VMEM((1, lanes), i32),
            pltpu.VMEM((2, lanes), f32),
            pltpu.SMEM(contrast.shape[::-1], f32),
            pltpu.VMEM((MB, 1, lanes), i32),
            pltpu.VMEM((MB, 2, 1, lanes), f32),
            pltpu.VMEM((2, rows, lanes), f32),
            pltpu.VMEM((2, rows, lanes), bf16),
            pltpu.VMEM((SENDS, face, lanes), bf16),
            pltpu.VMEM((SENDS, face, lanes), bf16),
            pltpu.VMEM((SENDS, face, lanes), bf16),
            pltpu.VMEM((SENDS, face, lanes), bf16),
            pltpu.VMEM((rows, lanes), f32),
            pltpu.VMEM((2 * rows, lanes), f32),
            pltpu.SemaphoreType.DMA((2,)),
            pltpu.SemaphoreType.DMA((4,)),
            pltpu.SemaphoreType.DMA((2, SENDS, CHUNKS)),
            pltpu.SemaphoreType.DMA((2, SENDS, CHUNKS)),
        ],
        compiler_params=pltpu.CompilerParams(collective_id=0, has_side_effects=True),
    )(
        green_ops[0, 0],
        cell_map.reshape(rows // lanes, lanes),
        dipole_site.reshape(1, lanes),
        dipole_amp[0, 0],
        contrast.T,
    )
    return out.reshape(1, 1, rows, 2, lanes)


def solution(mesh):
    placed = (
        P("gx", "gy", None, None, None),
        P("gx", "gy", None),
        P("gx", "gy", None),
        P("gx", "gy", None, None),
        P(),
    )
    return jax.shard_map(
        functools.partial(per_device, mesh.shape["gx"], mesh.shape["gy"]),
        mesh=mesh,
        in_specs=placed,
        out_specs=P("gx", "gy", None, None, None),
        check_vma=False,
    )
```

time: 52.8 us -> 24.5 us (0.46)
  waiting for transfers between devices: 23 us -> 0 us
  Pallas kernels: 0 us -> 22.1 us
  starting transfers between devices: 14 us -> 0 us
  matrix products: 8.72 us -> 0 us
  other arithmetic: 3.43 us -> 0 us
  local copies, waits for them, and re-layouts: 2.95 us -> 2.2 us
    ppermute x6 -> x0, waiting for transfers between devices: 23 us -> none  [from_behind(): return lax.ppermute(block, axis, route)]
    pallas_call x0 -> x1, Pallas kernels: none -> 22.1 us  [per_device(): pl.pallas_call(functools.partial(kernel, nx, ny), out_shape=jax.ShapeDtyp...]
    ppermute x6 -> x0, starting transfers between devices: 14 us -> none  [from_behind(): return lax.ppermute(block, axis, route)]
    dot_general x5 -> x0, matrix products: 8.72 us -> none  [the longest x4 7.59 us: per_device(): jnp.einsum('spq,qc->spc', operator, flat, preferred_element_type=jnp.floa...]
    another operation x1 -> x0, local copies, waits for them, and re-layouts: 1.33 us -> none  [combine(): return jnp.stack([real_out, imag_out], axis=1).astype(jnp.bfloat16)]
    another operation x13 -> x0, other arithmetic: 1.21 us -> none
    convert_element_type x4 -> x0, other arithmetic: 1.07 us -> none  [the longest x1 0.76 us: per_device(): (lax.broadcasted_iota(jnp.int32, (trace_rows, columns), 0) == sites[None,...]
    mul x1 -> x0, other arithmetic: 0.81 us -> none  [per_device(): source = one_hot[:, None, :] * amplitude[None, :, :]]
  transfers between devices with their start and end apart: 6 -> 0, of which waited for: 3 -> 0; matrix products, arithmetic and copies ran while one was open for 0% -> 0% of each run, Pallas kernels for 0% -> 0%
where the time goes in v1:
time: 24.5 us; the launch traced here: 24.3 us
  Pallas kernels  22.1 us (90%)
  local copies, waits for them, and re-layouts  2.2 us (9%)
    pallas_call x1, Pallas kernels, per_device(): pl.pallas_call(functools.partial(kernel, nx, ny), out_shape=jax.ShapeDtyp...  22.1 us
    unnamed x1, local copies, waits for them, and re-layouts  2.2 us

profile of v1, /device:TPU:8, one launch (start us, length us, event | category | flops | bytes accessed | tf_op | source)
XLA Modules:
  0.0 24.3 jit_solution(11421298880177394903)
XLA Ops:
  0.0 22.1 %shard_map.55 = bf16[2048,128]{1,0:T(8,128)(2,1)} custom-call(bf16[2,1024,1024]{2,1,0:T(8,128)(2,1)} %bitcast.6, s32[8,128]{1,0:T(8,128)} %bitcast.8, s32[1,128]{1,0:T(1,128)} %bitcast.11, f32[2,128]{1,0:T(2,128)} %bitcast.9, f32[2,3]{1,0:T(2,128)} %bitcast.10), custom_call_target="tpu_custom_call" | custom-call | tf_op jit(solution)/shard_map/pallas_call | solution.py:202
  22.1 2.2 %copy.7 = bf16[1,1,1024,2,128]{4,3,2,1,0:T(2,128)(2,1)} copy(bf16[1,1,1024,2,128]{4,3,2,1,0:T(2,128)(2,1)} %bitcast.7) | data formatting | bytes 1048576

commit v2 on v1

--- a/solution.py
+++ b/solution.py
@@ -201,7 +201,7 @@
     bf16, f32, i32 = jnp.bfloat16, jnp.float32, jnp.int32
     out = pl.pallas_call(
         functools.partial(kernel, nx, ny),
-        out_shape=jax.ShapeDtypeStruct((2 * rows, lanes), bf16),
+        out_shape=pltpu.VMEM((2 * rows, lanes), bf16),
         in_specs=[pl.BlockSpec(memory_space=pl.ANY)] * 5,
         out_specs=pl.BlockSpec(memory_space=pltpu.VMEM),
         scratch_shapes=[

time: 24.5 us -> 22.3 us (0.910)
  local copies, waits for them, and re-layouts: 2.2 us -> 0.8 us
  Pallas kernels: 22.1 us -> 21.3 us
    unnamed x1, local copies, waits for them, and re-layouts: 2.2 us -> 0.8 us
    pallas_call x1, Pallas kernels: 22.1 us -> 21.3 us  [per_device(): pl.pallas_call(functools.partial(kernel, nx, ny), out_shape=pltpu.VMEM((2...]
where the time goes in v2:
time: 22.3 us; the launch traced here: 22.1 us
  Pallas kernels  21.3 us (96%)
  local copies, waits for them, and re-layouts  0.8 us (4%)
    pallas_call x1, Pallas kernels, per_device(): pl.pallas_call(functools.partial(kernel, nx, ny), out_shape=pltpu.VMEM((2...  21.3 us
    unnamed x1, local copies, waits for them, and re-layouts  0.8 us

profile of v2, /device:TPU:8, one launch (start us, length us, event | category | flops | bytes accessed | tf_op | source)
XLA Modules:
  0.0 22.1 jit_solution(16983898489621764032)
XLA Ops:
  0.0 21.3 %shard_map.55 = bf16[2048,128]{1,0:T(8,128)(2,1)S(1)} custom-call(bf16[2,1024,1024]{2,1,0:T(8,128)(2,1)} %bitcast.7, s32[8,128]{1,0:T(8,128)} %bitcast.8, s32[1,128]{1,0:T(1,128)} %bitcast.11, f32[2,128]{1,0:T(2,128)} %bitcast.9, f32[2,3]{1,0:T(2,128)} %bitcast.10), custom_call_target="tpu_custom_call" | custom-call | tf_op jit(solution)/shard_map/pallas_call | solution.py:202
  21.3 0.8 %copy.7 = bf16[1,1,1024,2,128]{4,3,2,1,0:T(2,128)(2,1)} copy(bf16[1,1,1024,2,128]{4,3,2,1,0:T(2,128)(2,1)S(1)} %bitcast.6) | data formatting | bytes 1048576

commit v3 on v2

v3 whole, which is shorter than its diff:
```python
import functools

import jax
import jax.numpy as jnp
from jax import lax
from jax.experimental import pallas as pl
from jax.experimental.pallas import tpu as pltpu
from jax.sharding import PartitionSpec as P

MB = 2
STEPS = 4
CHUNKS = 2
TURNS = MB * STEPS - 1
SENDS = TURNS - MB
MESH = pl.DeviceIdType.MESH


def kernel(
    nx, ny, ops_hbm, cells_hbm, site_hbm, amp_hbm, contrast_hbm, out_ref,
    ops, ops_t, cells, site, amp, contrast, site_col, amp_col, fac, first, excited, total,
    west, south, east_out, north_out, final, wide, ops_sem, small_sem, send_sem, recv_sem,
):
    i = lax.axis_index("gx")
    j = lax.axis_index("gy")
    rows = ops.shape[1]
    face = rows // 2
    lanes = site.shape[1]
    nb = lanes // 2
    piece = face // CHUNKS
    bf16, f32 = jnp.bfloat16, jnp.float32
    bases = (face, 0)

    def ops_copy(direction, part):
        block = pl.ds(bases[direction] + part * piece, piece)
        return pltpu.make_async_copy(
            ops_hbm.at[:, block], ops.at[:, block], ops_sem.at[direction, part]
        )

    small = [
        pltpu.make_async_copy(src, dst, small_sem.at[k])
        for k, (src, dst) in enumerate(
            [(site_hbm, site), (amp_hbm, amp), (cells_hbm, cells), (contrast_hbm, contrast)]
        )
    ]
    for copy in small:
        copy.start()
    for direction in range(2):
        for part in range(CHUNKS):
            ops_copy(direction, part).start()

    barrier = pltpu.get_barrier_semaphore()

    @pl.when(i > 0)
    def _():
        pl.semaphore_signal(barrier, inc=1, device_id={"gx": i - 1}, device_id_type=MESH)

    @pl.when(j > 0)
    def _():
        pl.semaphore_signal(barrier, inc=1, device_id={"gy": j - 1}, device_id_type=MESH)

    for copy in small:
        copy.wait()

    low = lax.broadcasted_iota(jnp.int32, (1, lanes), 1) < nb
    sites = site[...]
    sites_turned = pltpu.roll(sites, nb, axis=1)
    real, imag = amp[0:1, :], amp[1:2, :]
    real_turned, imag_turned = pltpu.roll(real, nb, axis=1), pltpu.roll(imag, nb, axis=1)
    site_row = (jnp.where(low, sites, sites_turned), jnp.where(low, sites_turned, sites))
    amp_row = (jnp.where(low, real, imag_turned), jnp.where(low, real_turned, imag))
    turned_row = (jnp.where(low, -imag, real_turned), jnp.where(low, -imag_turned, real))
    for a in range(rows // lanes):
        block = pl.ds(a * lanes, lanes)
        points = lax.broadcasted_iota(jnp.int32, (lanes, lanes), 0) + a * lanes
        for m in range(MB):
            hit = points == site_row[m]
            columns = pl.ds(m * lanes, lanes)
            first[0, block, columns] = jnp.where(hit, amp_row[m], 0.0).astype(bf16)
            first[1, block, columns] = jnp.where(hit, turned_row[m], 0.0).astype(bf16)

    targets = jnp.where(i < nx - 1, 1, 0) + jnp.where(j < ny - 1, 1, 0)

    @pl.when(targets > 0)
    def _():
        pl.semaphore_wait(barrier, targets)

    def send(direction, turn, part):
        source, target, to = (
            (north_out, south, {"gy": j + 1}) if direction == 0 else (east_out, west, {"gx": i + 1})
        )
        return pltpu.make_async_remote_copy(
            src_ref=source.at[turn, part],
            dst_ref=target.at[turn, part],
            send_sem=send_sem.at[direction, turn, part],
            recv_sem=recv_sem.at[direction, turn, part],
            device_id=to,
            device_id_type=MESH,
        )

    has_target = (j < ny - 1, i < nx - 1)
    has_source = (j > 0, i > 0)

    for direction in range(2):
        held = (north_out, east_out)[direction]
        for part in range(CHUNKS):
            ops_copy(direction, part).wait()
            block = pl.ds(bases[direction] + part * piece, piece)
            image = jnp.dot(ops[0, block, :], first[0], preferred_element_type=f32) + jnp.dot(
                ops[1, block, :], first[1], preferred_element_type=f32
            )
            for m in range(MB):
                held[m, part] = image[:, m * lanes : (m + 1) * lanes].T.astype(bf16)

            @pl.when(has_target[direction])
            def _():
                send(direction, 0, part).start()

        @pl.when(has_target[direction])
        def _():
            for part in range(CHUNKS):
                send(direction, 1, part).start()

    @pl.when(i == 0)
    def _():
        west[...] = jnp.zeros_like(west)

    @pl.when(j == 0)
    def _():
        south[...] = jnp.zeros_like(south)

    for m in range(MB):
        site_col[m] = jnp.broadcast_to(site_row[m], (lanes, lanes)).T
        amp_col[m] = jnp.broadcast_to(amp_row[m], (lanes, lanes)).T
    for c in range(2):
        value = jnp.full(cells.shape, contrast[c, 0], f32)
        for k in range(1, contrast.shape[1]):
            value = jnp.where(cells[...] == k, contrast[c, k], value)
        fac[c] = value
    for c in range(2):
        for a in range(rows // lanes):
            block = pl.ds(a * lanes, lanes)
            ops_t[c, :, block] = ops[c, block, :].T

    def excite(m, buffer, slot, base):
        for a in range(face // lanes):
            part, inner = divmod(a * lanes, piece)
            x = buffer[slot, part, :, pl.ds(inner, lanes)].astype(f32)
            row = base // lanes + a
            fr, fi = fac[0, pl.ds(row, 1), :], fac[1, pl.ds(row, 1), :]
            points = lax.broadcasted_iota(jnp.int32, (lanes, lanes), 1) + row * lanes
            source = jnp.where(points == site_col[m], amp_col[m], 0.0)
            y_real = (fr * x[:nb] - fi * x[nb:] + source[:nb]).astype(bf16)
            y_imag = (fr * x[nb:] + fi * x[:nb] + source[nb:]).astype(bf16)
            block = pl.ds(base + a * lanes, lanes)
            excited[0, :nb, block] = y_real
            excited[0, nb:, block] = y_imag
            excited[1, :nb, block] = -y_imag
            excited[1, nb:, block] = y_real

    def product(depth, columns):
        return jnp.dot(
            excited[0, :, depth], ops_t[0, depth, columns], preferred_element_type=f32
        ) + jnp.dot(excited[1, :, depth], ops_t[1, depth, columns], preferred_element_type=f32)

    def turn_body(turn, _):
        m = turn % MB
        slot = turn - MB

        @pl.when(has_source[1])
        def _():
            for part in range(CHUNKS):
                send(1, slot, part).wait_recv()

        excite(m, west, slot, 0)
        total[...] = product(slice(0, face), slice(0, rows))

        @pl.when(has_source[0])
        def _():
            for part in range(CHUNKS):
                send(0, slot, part).wait_recv()

        excite(m, south, slot, face)
        for direction in range(2):
            held = (north_out, east_out)[direction]
            for part in range(CHUNKS):
                start = bases[direction] + part * piece
                columns = slice(start, start + piece)
                image = total[:, columns] + product(slice(face, rows), columns)

                @pl.when(turn < SENDS)
                def _():
                    held[turn, part] = image.astype(bf16)

                    @pl.when(has_target[direction])
                    def _():
                        send(direction, turn, part).start()

                @pl.when(turn == TURNS - 2)
                def _():
                    final[0, nb:, columns] = image[:nb]
                    final[1, nb:, columns] = image[nb:]

                @pl.when(turn == TURNS - 1)
                def _():
                    final[0, :nb, columns] = image[:nb]
                    final[1, :nb, columns] = image[nb:]
                    for a in range(start, start + piece, lanes):
                        for c in range(2):
                            wide[pl.ds(2 * a + c, lanes, stride=2), :] = final[c, :, a : a + lanes].T
                        both = pl.ds(2 * a, 2 * lanes)
                        out_ref[both, :] = wide[both, :].astype(bf16)

        return 0

    lax.fori_loop(MB, TURNS, turn_body, 0)

    for direction in (0, 1):
        @pl.when(has_target[direction])
        def _():
            for turn in range(SENDS):
                for part in range(CHUNKS):
                    send(direction, turn, part).wait_send()


def per_device(nx, ny, green_ops, cell_map, dipole_site, dipole_amp, contrast):
    rows = green_ops.shape[-1]
    lanes = dipole_site.shape[-1]
    face = rows // 2
    bf16, f32, i32 = jnp.bfloat16, jnp.float32, jnp.int32
    out = pl.pallas_call(
        functools.partial(kernel, nx, ny),
        out_shape=pltpu.VMEM((2 * rows, lanes), bf16),
        in_specs=[pl.BlockSpec(memory_space=pl.ANY)] * 5,
        out_specs=pl.BlockSpec(memory_space=pltpu.VMEM),
        scratch_shapes=[
            pltpu.VMEM((2, rows, rows), bf16),
            pltpu.VMEM((2, rows, rows), bf16),
            pltpu.VMEM((rows // lanes, lanes), i32),
            pltpu.VMEM((1, lanes), i32),
            pltpu.VMEM((2, lanes), f32),
            pltpu.SMEM(contrast.shape[::-1], f32),
            pltpu.VMEM((MB, lanes, lanes), i32),
            pltpu.VMEM((MB, lanes, lanes), f32),
            pltpu.VMEM((2, rows // lanes, lanes), f32),
            pltpu.VMEM((2, rows, MB * lanes), bf16),
            pltpu.VMEM((2, lanes, rows), bf16),
            pltpu.VMEM((lanes, rows), f32),
            *[pltpu.VMEM((SENDS, CHUNKS, lanes, face // CHUNKS), bf16)] * 4,
            pltpu.VMEM((2, lanes, rows), f32),
            pltpu.VMEM((2 * rows, lanes), f32),
            pltpu.SemaphoreType.DMA((2, CHUNKS)),
            pltpu.SemaphoreType.DMA((4,)),
            pltpu.SemaphoreType.DMA((2, SENDS, CHUNKS)),
            pltpu.SemaphoreType.DMA((2, SENDS, CHUNKS)),
        ],
        compiler_params=pltpu.CompilerParams(collective_id=0, has_side_effects=True),
    )(
        green_ops[0, 0],
        cell_map.reshape(rows // lanes, lanes),
        dipole_site.reshape(1, lanes),
        dipole_amp[0, 0],
        contrast.T,
    )
    return out.reshape(1, 1, rows, 2, lanes)


def solution(mesh):
    placed = (
        P("gx", "gy", None, None, None),
        P("gx", "gy", None),
        P("gx", "gy", None),
        P("gx", "gy", None, None),
        P(),
    )
    return jax.shard_map(
        functools.partial(per_device, mesh.shape["gx"], mesh.shape["gy"]),
        mesh=mesh,
        in_specs=placed,
        out_specs=P("gx", "gy", None, None, None),
        check_vma=False,
    )
```

time: 22.3 us -> 21.9 us (0.982)
  Pallas kernels: 21.3 us -> 21 us
    pallas_call x1, Pallas kernels: 21.3 us -> 21 us  [per_device(): pl.pallas_call(functools.partial(kernel, nx, ny), out_shape=pltpu.VMEM((2...]
where the time goes in v3:
time: 21.9 us; the launch traced here: 21.8 us
  Pallas kernels  21 us (96%)
  local copies, waits for them, and re-layouts  0.8 us (4%)
    pallas_call x1, Pallas kernels, per_device(): pl.pallas_call(functools.partial(kernel, nx, ny), out_shape=pltpu.VMEM((2...  21 us
    unnamed x1, local copies, waits for them, and re-layouts  0.8 us

profile of v3, /device:TPU:8, one launch (start us, length us, event | category | flops | bytes accessed | tf_op | source)
XLA Modules:
  0.0 21.8 jit_solution(12300753956059048000)
XLA Ops:
  0.0 21.0 %shard_map.55 = bf16[2048,128]{1,0:T(8,128)(2,1)S(1)} custom-call(bf16[2,1024,1024]{2,1,0:T(8,128)(2,1)} %bitcast.7, s32[8,128]{1,0:T(8,128)} %bitcast.8, s32[1,128]{1,0:T(1,128)} %bitcast.11, f32[2,128]{1,0:T(2,128)} %bitcast.9, f32[2,3]{1,0:T(2,128)} %bitcast.10), custom_call_target="tpu_custom_call" | custom-call | tf_op jit(solution)/shard_map/pallas_call | solution.py:230
  21.0 0.8 %copy.7 = bf16[1,1,1024,2,128]{4,3,2,1,0:T(2,128)(2,1)} copy(bf16[1,1,1024,2,128]{4,3,2,1,0:T(2,128)(2,1)S(1)} %bitcast.6) | data formatting | bytes 1048576

commit v4 on v3

--- a/solution.py
+++ b/solution.py
@@ -18,7 +18,7 @@
 def kernel(
     nx, ny, ops_hbm, cells_hbm, site_hbm, amp_hbm, contrast_hbm, out_ref,
     ops, ops_t, cells, site, amp, contrast, site_col, amp_col, fac, first, excited, total,
-    west, south, east_out, north_out, final, wide, ops_sem, small_sem, send_sem, recv_sem,
+    west, south, east_out, north_out, final, order, ops_sem, small_sem, send_sem, recv_sem,
 ):
     i = lax.axis_index("gx")
     j = lax.axis_index("gy")
@@ -58,7 +58,7 @@
     def _():
         pl.semaphore_signal(barrier, inc=1, device_id={"gy": j - 1}, device_id_type=MESH)
 
-    for copy in small:
+    for copy in small[:2]:
         copy.wait()
 
     low = lax.broadcasted_iota(jnp.int32, (1, lanes), 1) < nb
@@ -108,8 +108,9 @@
             image = jnp.dot(ops[0, block, :], first[0], preferred_element_type=f32) + jnp.dot(
                 ops[1, block, :], first[1], preferred_element_type=f32
             )
+            image = image.astype(bf16)
             for m in range(MB):
-                held[m, part] = image[:, m * lanes : (m + 1) * lanes].T.astype(bf16)
+                held[m, part] = image[:, m * lanes : (m + 1) * lanes].T
 
             @pl.when(has_target[direction])
             def _():
@@ -119,6 +120,12 @@
         def _():
             for part in range(CHUNKS):
                 send(direction, 1, part).start()
+
+    for copy in small[2:]:
+        copy.wait()
+    row = lax.broadcasted_iota(jnp.int32, order.shape, 0)
+    column = lax.broadcasted_iota(jnp.int32, order.shape, 1)
+    order[...] = jnp.where(column == (row % 2) * lanes + row // 2, 1.0, 0.0).astype(bf16)
 
     @pl.when(i == 0)
     def _():
@@ -141,10 +148,9 @@
             block = pl.ds(a * lanes, lanes)
             ops_t[c, :, block] = ops[c, block, :].T
 
-    def excite(m, buffer, slot, base):
-        for a in range(face // lanes):
-            part, inner = divmod(a * lanes, piece)
-            x = buffer[slot, part, :, pl.ds(inner, lanes)].astype(f32)
+    def excite(m, buffer, slot, part, base):
+        for a in range(piece // lanes):
+            x = buffer[slot, part, :, pl.ds(a * lanes, lanes)].astype(f32)
             row = base // lanes + a
             fr, fi = fac[0, pl.ds(row, 1), :], fac[1, pl.ds(row, 1), :]
             points = lax.broadcasted_iota(jnp.int32, (lanes, lanes), 1) + row * lanes
@@ -162,7 +168,7 @@
             excited[0, :, depth], ops_t[0, depth, columns], preferred_element_type=f32
         ) + jnp.dot(excited[1, :, depth], ops_t[1, depth, columns], preferred_element_type=f32)
 
-    def turn_body(turn, _):
+    def gather(turn):
         m = turn % MB
         slot = turn - MB
 
@@ -171,48 +177,62 @@
             for part in range(CHUNKS):
                 send(1, slot, part).wait_recv()
 
-        excite(m, west, slot, 0)
+        for part in range(CHUNKS):
+            excite(m, west, slot, part, part * piece)
         total[...] = product(slice(0, face), slice(0, rows))
-
-        @pl.when(has_source[0])
-        def _():
-            for part in range(CHUNKS):
+        for part in range(CHUNKS):
+            @pl.when(has_source[0])
+            def _():
                 send(0, slot, part).wait_recv()
 
-        excite(m, south, slot, face)
+            start = face + part * piece
+            excite(m, south, slot, part, start)
+            if part < CHUNKS - 1:
+                total[...] += product(slice(start, start + piece), slice(0, rows))
+
+    last_piece = slice(rows - piece, rows)
+
+    def turn_body(turn, _):
+        gather(turn)
         for direction in range(2):
             held = (north_out, east_out)[direction]
-            for part in range(CHUNKS):
-                start = bases[direction] + part * piece
-                columns = slice(start, start + piece)
-                image = total[:, columns] + product(slice(face, rows), columns)
-
-                @pl.when(turn < SENDS)
+            columns = slice(bases[direction], bases[direction] + face)
+            image = (total[:, columns] + product(last_piece, columns)).astype(bf16)
+
+            @pl.when(turn < SENDS)
+            def _():
+                for part in range(CHUNKS):
+                    held[turn, part] = image[:, part * piece : (part + 1) * piece]
+
+                @pl.when(has_target[direction])
                 def _():
-                    held[turn, part] = image.astype(bf16)
-
-                    @pl.when(has_target[direction])
-                    def _():
+                    for part in range(CHUNKS):
                         send(direction, turn, part).start()
 
-                @pl.when(turn == TURNS - 2)
-                def _():
-                    final[0, nb:, columns] = image[:nb]
-                    final[1, nb:, columns] = image[nb:]
-
-                @pl.when(turn == TURNS - 1)
-                def _():
-                    final[0, :nb, columns] = image[:nb]
-                    final[1, :nb, columns] = image[nb:]
-                    for a in range(start, start + piece, lanes):
-                        for c in range(2):
-                            wide[pl.ds(2 * a + c, lanes, stride=2), :] = final[c, :, a : a + lanes].T
-                        both = pl.ds(2 * a, 2 * lanes)
-                        out_ref[both, :] = wide[both, :].astype(bf16)
+            @pl.when(turn == TURNS - 2)
+            def _():
+                final[0, nb:, columns] = image[:nb]
+                final[1, nb:, columns] = image[nb:]
 
         return 0
 
-    lax.fori_loop(MB, TURNS, turn_body, 0)
+    lax.fori_loop(MB, TURNS - 1, turn_body, 0)
+
+    gather(TURNS - 1)
+    for start in range(0, rows, 2 * lanes):
+        columns = slice(start, start + 2 * lanes)
+        image = (total[:, columns] + product(last_piece, columns)).astype(bf16)
+        for a in range(2):
+            part = slice(a * lanes, (a + 1) * lanes)
+            block = slice(start + a * lanes, start + (a + 1) * lanes)
+            real = jnp.concatenate([image[:nb, part], final[0, nb:, block]], axis=0)
+            imag = jnp.concatenate([image[nb:, part], final[1, nb:, block]], axis=0)
+            out_ref[pl.ds(2 * (start + a * lanes), 2 * lanes), :] = lax.dot_general(
+                order[...],
+                jnp.concatenate([real, imag], axis=1),
+                (((1,), (1,)), ((), ())),
+                preferred_element_type=f32,
+            ).astype(bf16)
 
     for direction in (0, 1):
         @pl.when(has_target[direction])
@@ -246,8 +266,8 @@
             pltpu.VMEM((2, lanes, rows), bf16),
             pltpu.VMEM((lanes, rows), f32),
             *[pltpu.VMEM((SENDS, CHUNKS, lanes, face // CHUNKS), bf16)] * 4,
-            pltpu.VMEM((2, lanes, rows), f32),
-            pltpu.VMEM((2 * rows, lanes), f32),
+            pltpu.VMEM((2, lanes, rows), bf16),
+            pltpu.VMEM((2 * lanes, 2 * lanes), bf16),
             pltpu.SemaphoreType.DMA((2, CHUNKS)),
             pltpu.SemaphoreType.DMA((4,)),
             pltpu.SemaphoreType.DMA((2, SENDS, CHUNKS)),

time: 21.9 us -> 21.4 us (0.977)
  Pallas kernels: 21 us -> 20.4 us
    pallas_call x1, Pallas kernels: 21 us -> 20.4 us  [per_device(): pl.pallas_call(functools.partial(kernel, nx, ny), out_shape=pltpu.VMEM((2...]
where the time goes in v4:
time: 21.4 us; the launch traced here: 21.2 us
  Pallas kernels  20.4 us (95%)
  local copies, waits for them, and re-layouts  0.8 us (4%)
    pallas_call x1, Pallas kernels, per_device(): pl.pallas_call(functools.partial(kernel, nx, ny), out_shape=pltpu.VMEM((2...  20.4 us
    unnamed x1, local copies, waits for them, and re-layouts  0.8 us

profile of v4, /device:TPU:8, one launch (start us, length us, event | category | flops | bytes accessed | tf_op | source)
XLA Modules:
  0.0 21.2 jit_solution(8616150327433253170)
XLA Ops:
  0.0 20.4 %shard_map.55 = bf16[2048,128]{1,0:T(8,128)(2,1)S(1)} custom-call(bf16[2,1024,1024]{2,1,0:T(8,128)(2,1)} %bitcast.7, s32[8,128]{1,0:T(8,128)} %bitcast.8, s32[1,128]{1,0:T(1,128)} %bitcast.11, f32[2,128]{1,0:T(2,128)} %bitcast.9, f32[2,3]{1,0:T(2,128)} %bitcast.10), custom_call_target="tpu_custom_call" | custom-call | tf_op jit(solution)/shard_map/pallas_call | solution.py:250
  20.4 0.8 %copy.7 = bf16[1,1,1024,2,128]{4,3,2,1,0:T(2,128)(2,1)} copy(bf16[1,1,1024,2,128]{4,3,2,1,0:T(2,128)(2,1)S(1)} %bitcast.6) | data formatting | bytes 1048576

commit v5 on v4

--- a/solution.py
+++ b/solution.py
@@ -219,20 +219,17 @@
     lax.fori_loop(MB, TURNS - 1, turn_body, 0)
 
     gather(TURNS - 1)
-    for start in range(0, rows, 2 * lanes):
-        columns = slice(start, start + 2 * lanes)
-        image = (total[:, columns] + product(last_piece, columns)).astype(bf16)
-        for a in range(2):
-            part = slice(a * lanes, (a + 1) * lanes)
-            block = slice(start + a * lanes, start + (a + 1) * lanes)
-            real = jnp.concatenate([image[:nb, part], final[0, nb:, block]], axis=0)
-            imag = jnp.concatenate([image[nb:, part], final[1, nb:, block]], axis=0)
-            out_ref[pl.ds(2 * (start + a * lanes), 2 * lanes), :] = lax.dot_general(
-                order[...],
-                jnp.concatenate([real, imag], axis=1),
-                (((1,), (1,)), ((), ())),
-                preferred_element_type=f32,
-            ).astype(bf16)
+    image = (total[...] + product(last_piece, slice(0, rows))).astype(bf16)
+    for a in range(rows // lanes):
+        block = slice(a * lanes, (a + 1) * lanes)
+        real = jnp.concatenate([image[:nb, block], final[0, nb:, block]], axis=0)
+        imag = jnp.concatenate([image[nb:, block], final[1, nb:, block]], axis=0)
+        out_ref[pl.ds(2 * a * lanes, 2 * lanes), :] = lax.dot_general(
+            order[...],
+            jnp.concatenate([real, imag], axis=1),
+            (((1,), (1,)), ((), ())),
+            preferred_element_type=f32,
+        ).astype(bf16)
 
     for direction in (0, 1):
         @pl.when(has_target[direction])

time: 21.4 us -> 20.8 us (0.972)
  Pallas kernels: 20.4 us -> 19.9 us
    pallas_call x1, Pallas kernels: 20.4 us -> 19.9 us  [per_device(): pl.pallas_call(functools.partial(kernel, nx, ny), out_shape=pltpu.VMEM((2...]
where the time goes in v5:
time: 20.8 us; the launch traced here: 20.7 us
  Pallas kernels  19.9 us (96%)
  local copies, waits for them, and re-layouts  0.8 us (4%)
    pallas_call x1, Pallas kernels, per_device(): pl.pallas_call(functools.partial(kernel, nx, ny), out_shape=pltpu.VMEM((2...  19.9 us
    unnamed x1, local copies, waits for them, and re-layouts  0.8 us

profile of v5, /device:TPU:8, one launch (start us, length us, event | category | flops | bytes accessed | tf_op | source)
XLA Modules:
  0.0 20.7 jit_solution(13094803173098226655)
XLA Ops:
  0.0 19.9 %shard_map.55 = bf16[2048,128]{1,0:T(8,128)(2,1)S(1)} custom-call(bf16[2,1024,1024]{2,1,0:T(8,128)(2,1)} %bitcast.7, s32[8,128]{1,0:T(8,128)} %bitcast.8, s32[1,128]{1,0:T(1,128)} %bitcast.11, f32[2,128]{1,0:T(2,128)} %bitcast.9, f32[2,3]{1,0:T(2,128)} %bitcast.10), custom_call_target="tpu_custom_call" | custom-call | tf_op jit(solution)/shard_map/pallas_call | solution.py:247
  19.9 0.8 %copy.7 = bf16[1,1,1024,2,128]{4,3,2,1,0:T(2,128)(2,1)} copy(bf16[1,1,1024,2,128]{4,3,2,1,0:T(2,128)(2,1)S(1)} %bitcast.6) | data formatting | bytes 1048576
